TPU v7x, 256 devices: a whole 4x4x8 slice. The times are simulated.
256 devices in a mesh: left: 16 (over z, y_hi), right: 16 (over y_lo, x, core).
Axes of the slice: x: 4, y: 4 (y_hi: 2, y_lo: 2; y = y_hi * 2 + y_lo), z: 8, core: 2. Of those that a mesh axis runs over, the one named last changes fastest.
Arguments:
- left_table: float32 [32768, 400], P(('left', 'right')), may hold values from -2 to 2
- left_state: float32 [32768], P(('left', 'right')), may hold values from 0.05 to 0.5
- right_table: float32 [32768, 400], P(('left', 'right')), may hold values from -2 to 2
- right_state: float32 [32768], P(('left', 'right')), may hold values from 0.05 to 0.5
- relation_table: float32 [256, 400], replicated, may hold values from -6 to 6
- relation_state: float32 [256], replicated, may hold values from 0.05 to 0.5
- source_ids: int32 [16, 16, 1024], P('left', 'right'), may hold values from 0 to 2047
- target_ids: int32 [16, 16, 1024], P('left', 'right'), may hold values from 0 to 2047
- relation_ids: int32 [16, 16, 1024], P('left', 'right'), may hold values from 0 to 255
- negative_ids: int32 [16, 16, 2, 1024], P('left', 'right'), may hold values from 0 to 2047
Outputs:
- left_new: float32 [32768, 400], P(('left', 'right'))
- left_state_new: float32 [32768], P(('left', 'right'))
- right_new: float32 [32768, 400], P(('left', 'right'))
- right_state_new: float32 [32768], P(('left', 'right'))
- relation_new: float32 [256, 400], replicated
- relation_state_new: float32 [256], replicated
All inputs are finite; a program needn't handle non-finite values.
Results may differ from a plain program's by a relative error of at most 0.0021.
Values may be sent and summed in bfloat16 or wider, within the bound.
A program may use at most 64 MiB of HBM per device.

v0:
```python
import jax
import jax.numpy as jnp
from jax import lax
from jax.sharding import PartitionSpec as P

LEARN_RATE = 0.1
NEG_WEIGHT = 0.03125


def from_behind(value, axis, by):
    devices = lax.axis_size(axis)
    return lax.ppermute(value, axis, [(i, (i + by) % devices) for i in range(devices)])


def complex_product(first, second):
    half_width = first.shape[-1] // 2
    a_re, a_im = (first[..., :half_width], first[..., half_width:])
    b_re, b_im = (second[..., :half_width], second[..., half_width:])
    return jnp.concatenate([a_re * b_re - a_im * b_im, a_re * b_im + a_im * b_re], axis=-1)


def complex_back(grad, other):
    half_width = grad.shape[-1] // 2
    g_re, g_im = (grad[..., :half_width], grad[..., half_width:])
    o_re, o_im = (other[..., :half_width], other[..., half_width:])
    return jnp.concatenate([g_re * o_re + g_im * o_im, g_im * o_re - g_re * o_im], axis=-1)


def adagrad(table, state, grad):
    state_new = state + jnp.mean(grad * grad, axis=-1)
    return (table - LEARN_RATE * grad / jnp.sqrt(state_new)[:, None], state_new)


def one_hot_rows(ids, count):
    columns = jnp.arange(count, dtype=jnp.int32)
    return (ids[:, None] == columns[None, :]).astype(jnp.bfloat16)


def per_device(
    left_table,
    left_state,
    right_table,
    right_state,
    relation_table,
    relation_state,
    source_ids,
    target_ids,
    relation_ids,
    negative_ids,
):
    row_count = left_table.shape[0]
    width = left_table.shape[1]
    source = source_ids.reshape(-1)
    target = target_ids.reshape(-1)
    relation = relation_ids.reshape(-1)
    negative = negative_ids.reshape(negative_ids.shape[2], negative_ids.shape[3])
    groups = negative.shape[0]
    edge_count = source.shape[0]
    moved_table, moved_state = from_behind((right_table, right_state), "right", 1)
    right_part = lax.all_gather(moved_table.astype(jnp.bfloat16), "left", axis=0, tiled=True)
    piece = lax.all_gather(left_table.astype(jnp.bfloat16), "right", axis=0, tiled=True)
    onehot = one_hot_rows(source, piece.shape[0])
    source_emb = jnp.dot(onehot, piece, preferred_element_type=jnp.float32)
    target_hot = one_hot_rows(target, right_part.shape[0])
    target_embedding = jnp.dot(target_hot, right_part, preferred_element_type=jnp.float32)
    relation_bf = relation_table.astype(jnp.bfloat16)
    relation_hot = one_hot_rows(relation, relation_table.shape[0])
    relation_emb = jnp.dot(relation_hot, relation_bf, preferred_element_type=jnp.float32)
    query = complex_product(source_emb, relation_emb)
    positive = jnp.sum(query * target_embedding, axis=-1)
    query_block_rows = query.astype(jnp.bfloat16).reshape(groups, -1, width)
    negative_rows = jnp.take(right_part, negative, axis=0)
    score_matrix = jnp.einsum(
        "wet,wjt->wej", query_block_rows, negative_rows, preferred_element_type=jnp.float32
    )
    positive_score_grad = -jax.nn.sigmoid(-positive)
    negative_score_grad = (NEG_WEIGHT * jax.nn.sigmoid(score_matrix)).astype(jnp.bfloat16)
    from_negatives = jnp.einsum(
        "fjs,fsh->fjh", negative_score_grad, negative_rows, preferred_element_type=jnp.float32
    )
    query_gradient = positive_score_grad[:, None] * target_embedding + from_negatives.reshape(
        edge_count, width
    )
    negative_embedding_grad = (
        jnp.einsum(
            "fre,frl->fel",
            negative_score_grad,
            query_block_rows,
            preferred_element_type=jnp.float32,
        )
        .astype(jnp.bfloat16)
        .reshape(-1, width)
    )
    target_grad = (positive_score_grad[:, None] * query).astype(jnp.bfloat16)
    source_grad = complex_back(query_gradient, relation_emb).astype(jnp.bfloat16)
    relation_grad = complex_back(query_gradient, source_emb).astype(jnp.bfloat16)
    relation_term = jnp.einsum(
        "er,ed->rd", relation_hot, relation_grad, preferred_element_type=jnp.float32
    )
    onehot = one_hot_rows(source, lax.axis_size("right") * row_count)
    left_grad = lax.psum_scatter(
        jnp.einsum("er,ed->rd", onehot, source_grad, preferred_element_type=jnp.float32),
        "right",
        scatter_dimension=0,
        tiled=True,
    )
    all_ids = jnp.concatenate([target, negative.reshape(-1)])
    all_grads = jnp.concatenate([target_grad, negative_embedding_grad], axis=0)
    onehot = one_hot_rows(all_ids, lax.axis_size("left") * row_count)
    right_grad = lax.psum_scatter(
        jnp.einsum("er,ed->rd", onehot, all_grads, preferred_element_type=jnp.float32),
        "left",
        scatter_dimension=0,
        tiled=True,
    )
    left_new, left_state_new = adagrad(left_table, left_state, left_grad)
    right_new, right_state_new = adagrad(moved_table, moved_state, right_grad)
    relation_total = lax.psum(relation_term, ("left", "right"))
    relation_new, relation_state_new = adagrad(relation_table, relation_state, relation_total)
    return (left_new, left_state_new, right_new, right_state_new, relation_new, relation_state_new)


def solution(mesh):
    return jax.shard_map(
        per_device,
        mesh=mesh,
        in_specs=(
            P(("left", "right"), None),
            P(("left", "right")),
            P(("left", "right"), None),
            P(("left", "right")),
            P(),
            P(),
            P("left", "right", None),
            P("left", "right", None),
            P("left", "right", None),
            P("left", "right", None, None),
        ),
        out_specs=(
            P(("left", "right"), None),
            P(("left", "right")),
            P(("left", "right"), None),
            P(("left", "right")),
            P(),
            P(),
        ),
        check_vma=False,
    )
```

profile of v0, /device:TPU:2, one launch (start us, length us, event | category | flops | bytes accessed | tf_op | source)
XLA Modules:
  0.0 661.7 jit_solution(7649774851200412998)
XLA Ops:
  7.2 1.6 convert_element_type.13
  9.0 5.4 collective-permute-done
  16.5 1.5 fusion.13
  18.0 33.1 %all-gather.3.cloned.1.call-done = bf16[2048,400]{0,1:T(8,128)(2,1)} async-done(((bf16[128,400]{0,1:T(8,128)(2,1)}), bf16[2048,400]{0,1:T(8,128)(2,1)}) %all-gather.3.cloned.1.call-update) | async-done | bytes 1638416 | tf_op jit(solution)/shard_map/all_gather | solution.py:61
  51.1 3.5 fusion.3
  54.7 1.5 fusion.34
  57.2 77.7 %all-gather.5.cloned.1.call-done = bf16[2048,400]{0,1:T(8,128)(2,1)} async-done(((bf16[128,400]{0,1:T(8,128)(2,1)}), bf16[2048,400]{0,1:T(8,128)(2,1)}) %all-gather.5.cloned.1.call-update) | async-done | bytes 1638416 | tf_op jit(solution)/shard_map/all_gather | solution.py:60
  134.9 2.8 copy.24
  137.7 9.2 %gather_fusion = bf16[2048,400]{1,0:T(8,128)(2,1)} fusion(bf16[2048,400]{1,0:T(8,128)(2,1)S(1)} %copy.24, s32[2048]{0:T(1024)S(1)} %bitcast_clamp_fusion), kind=kCustom, calls=%fused_computation | custom fusion | bytes 3284992 | tf_op jit(solution)/shard_map/jit(_take)/gather | solution.py:72
  146.9 4.1 copy.25
  151.0 2.2 multiply_reduce_fusion
  153.2 1.8 multiply_convert_fusion
  155.0 1.0 convolution_bitcast_fusion
  159.2 1.3 fusion.12
  160.7 3.9 fusion.2
  165.7 2.6 fusion.11
  168.5 7.8 %fusion = f32[2048,400]{0,1:T(8,128)} fusion(s32[3072]{0:T(1024)S(1)} %pad_add_fusion, bf16[2048,400]{0,1:T(8,128)(2,1)S(1)} %bitcast.39, bf16[1024,400]{0,1:T(8,128)(2,1)S(1)} %get-tuple-element.24), kind=kOutput, calls=%fused_computation.2 | convolution fusion | flops 5044371456 | bytes 5746688 | tf_op jit(solution)/shard_map/er,ed->rd/dot_general | solution.py:111
  177.0 232.2 %all-reduce.2.cloned.1.call-done = f32[256,400]{0,1:T(8,128)} async-done(((f32[256,400]{0,1:T(8,128)}), f32[256,400]{0,1:T(8,128)}) %all-reduce.2.cloned.1.call-update) | async-done | bytes 409616 | tf_op jit(solution)/shard_map/psum | solution.py:118
  409.2 1.1 multiply_reduce_fusion.1
  410.8 1.8 divide_subtract_fusion
  412.6 61.2 %reduce-scatter.3.cloned.1.call-done = f32[128,400]{0,1:T(8,128)} async-done(((f32[2048,400]{0,1:T(8,128)}), f32[128,400]{0,1:T(8,128)}) %reduce-scatter.3.cloned.1.call-update) | async-done | bytes 204816 | tf_op jit(solution)/shard_map/reduce_scatter | solution.py:101
  475.3 175.1 %reduce-scatter.5.cloned.1.call-done = f32[128,400]{0,1:T(8,128)} async-done(((f32[2048,400]{0,1:T(8,128)}), f32[128,400]{0,1:T(8,128)}) %reduce-scatter.5.cloned.1.call-update) | async-done | bytes 204816 | tf_op jit(solution)/shard_map/reduce_scatter | solution.py:110
  651.9 1.6 divide_subtract_fusion.1
  653.5 1.6 divide_subtract_fusion.2
  (71 shorter events, 12.2 us)
Async XLA Ops:
  7.2 44.0 %copy-start.17 = (s32[1,1,1024]{2,1,0:T(1,128)S(1)}, s32[1,1,1024]{2,1,0:T(1,128)}, u32[]{:S(2)}) copy-start(s32[1,1,1024]{2,1,0:T(1,128)} %param.16) | copy-start | bytes 12292
  7.2 44.0 %all-gather.3.cloned.1.call-start = ((), (), s32[]{:S(2)}) async-start(), calls=%async_computation.2 | async-start | bytes 1740800 | tf_op jit(solution)/shard_map/all_gather | solution.py:61
  8.8 126.1 %all-gather.5.cloned.1.call-start = ((), (), s32[]{:S(2)}) async-start(), calls=%async_computation.3 | async-start | bytes 1740800 | tf_op jit(solution)/shard_map/all_gather | solution.py:60
  8.9 5.5 collective-permute-start
  15.0 394.1 %all-reduce.2.cloned.1.call-start = ((), (), s32[]{:S(2)}) async-start(), calls=%async_computation.6 | async-start | bytes 819200 | tf_op jit(solution)/shard_map/psum | solution.py:118
  18.0 36.7 %copy-start = (f32[1024,400]{0,1:T(8,128)}, f32[1024,400]{0,1:T(8,128)S(1)}, u32[]{:S(2)}) copy-start(f32[1024,400]{0,1:T(8,128)S(1)} %fusion.13) | copy-start | bytes 4915204
  54.7 1.5 copy-start.2
  56.3 1.0 copy-start.9
  146.9 4.1 copy-start.4
  146.9 4.1 copy-start.5
  146.9 4.1 copy-start.14
  151.0 2.2 copy-start.6
  151.0 2.2 copy-start.10
  155.0 1.3 copy-start.19
  156.5 1.4 copy-start.1
  156.5 1.9 copy-start.3
  160.4 313.4 %reduce-scatter.3.cloned.1.call-start = ((), (), s32[]{:S(2)}) async-start(), calls=%async_computation.4 | async-start | bytes 3481600 | tf_op jit(solution)/shard_map/reduce_scatter | solution.py:101
  164.6 1.2 copy-start.11
  164.6 485.8 %reduce-scatter.5.cloned.1.call-start = ((), (), s32[]{:S(2)}) async-start(), calls=%async_computation.5 | async-start | bytes 3481600 | tf_op jit(solution)/shard_map/reduce_scatter | solution.py:110
  176.3 233.9 %copy-start.15 = (f32[256]{0:T(256)S(1)}, f32[256]{0:T(256)}, u32[]{:S(2)}) copy-start(f32[256]{0:T(256)} %param.15) | copy-start | bytes 3076
  176.3 234.5 %copy-start.7 = (f32[256,400]{0,1:T(8,128)S(1)}, f32[256,400]{0,1:T(8,128)}, u32[]{:S(2)}) copy-start(f32[256,400]{0,1:T(8,128)} %param.14) | copy-start | bytes 1228804
  177.0 297.8 %copy-start.16 = (f32[128]{0:T(128)S(1)}, f32[128]{0:T(128)}, u32[]{:S(2)}) copy-start(f32[128]{0:T(128)} %param.11) | copy-start | bytes 1540
  177.0 476.5 %copy-start.8 = (f32[128,400]{0,1:T(8,128)S(1)}, f32[128,400]{0,1:T(8,128)}, u32[]{:S(2)}) copy-start(f32[128,400]{0,1:T(8,128)} %param.10) | copy-start | bytes 614404
  177.0 474.4 %collective-permute-start.1 = (f32[128]{0:T(128)S(1)}, f32[128]{0:T(128)S(1)}, u32[]{:S(2)}, u32[]{:S(2)}) collective-permute-start(f32[128]{0:T(128)S(1)} %copy-done.18), channel_id=1, source_target_pairs={{0,1},{1,2},{2,3},{3,4},{4,5},{5,6},{6,7},{7,8},{8,9},{9,10},{10,1... | collective-permute-start | bytes 1544 | tf_op jit(solution)/shard_map/ppermute | solution.py:12
  (3 other events, 2.0 us)
Sparse Core Ops, SparseCore 0:
  10.3 40.7 all-gather.2
  54.2 80.7 all-gather.4
  160.6 248.5 all-reduce.1
  411.6 62.1 reduce-scatter.2
  477.6 172.6 reduce-scatter.4
where the time goes:
time: 662 us
  waiting for transfers between devices  585 us (88%)
  matrix products  25.7 us (4%)
  local copies, waits for them, and re-layouts  20.5 us (3%)
  other arithmetic  16.3 us (2%)
  between operations  14 us (2%)
    psum x1, waiting for transfers between devices, per_device(): relation_total = lax.psum(relation_term, ('left', 'right'))  232 us
    reduce_scatter x1, waiting for transfers between devices, per_device(): lax.psum_scatter(jnp.einsum('er,ed->rd', onehot, all_grads, preferred_ele...  175 us
    all_gather x1, waiting for transfers between devices, per_device(): lax.all_gather(moved_table.astype(jnp.bfloat16), 'left', axis=0, tiled=True)  77.7 us
    reduce_scatter x1, waiting for transfers between devices, per_device(): lax.psum_scatter(jnp.einsum('er,ed->rd', onehot, source_grad, preferred_e...  61.2 us
    all_gather x1, waiting for transfers between devices, per_device(): lax.all_gather(left_table.astype(jnp.bfloat16), 'right', axis=0, tiled=True)  33.1 us
    gather x2, local copies, waits for them, and re-layouts, per_device(): negative_rows = jnp.take(right_part, negative, axis=0)  13.2 us
  transfers between devices with their start and end apart: 7, of which 6 were waited for; matrix products, arithmetic and copies ran while one was open for 4% of the time, Pallas kernels for 0%

commit v1 on v0

--- a/solution.py
+++ b/solution.py
@@ -58,7 +58,12 @@
     edge_count = source.shape[0]
     moved_table, moved_state = from_behind((right_table, right_state), "right", 1)
     right_part = lax.all_gather(moved_table.astype(jnp.bfloat16), "left", axis=0, tiled=True)
-    piece = lax.all_gather(left_table.astype(jnp.bfloat16), "right", axis=0, tiled=True)
+    piece = jnp.concatenate(
+        lax.all_to_all(
+            jnp.stack([left_table.astype(jnp.bfloat16)] * lax.axis_size("right")), "right", 0, 0
+        ),
+        axis=0,
+    )
     onehot = one_hot_rows(source, piece.shape[0])
     source_emb = jnp.dot(onehot, piece, preferred_element_type=jnp.float32)
     target_hot = one_hot_rows(target, right_part.shape[0])

time: 662 us -> 634 us (0.958)
  waiting for transfers between devices: 585 us -> 550 us
  starting transfers between devices: 0.47 us -> 9.05 us
    all_gather x1 -> x0, waiting for transfers between devices: 33.1 us -> none  [per_device(): lax.all_gather(left_table.astype(jnp.bfloat16), 'right', axis=0, tiled=True)]
    all_gather x1, waiting for transfers between devices: 77.7 us -> 54 us  [per_device(): lax.all_gather(moved_table.astype(jnp.bfloat16), 'left', axis=0, tiled=True)]
    all_to_all x0 -> x1, waiting for transfers between devices: none -> 21.4 us  [per_device(): lax.all_to_all(jnp.stack([left_table.astype(jnp.bfloat16)] * lax.axis_siz...]
    all_to_all x0 -> x1, starting transfers between devices: none -> 8.62 us  [per_device(): lax.all_to_all(jnp.stack([left_table.astype(jnp.bfloat16)] * lax.axis_siz...]
where the time goes in v1:
time: 634 us
  waiting for transfers between devices  550 us (87%)
  matrix products  24.6 us (4%)
  local copies, waits for them, and re-layouts  21.9 us (3%)
  other arithmetic  14.3 us (2%)
  between operations  14.1 us (2%)
  starting transfers between devices  9.05 us (1%)
    psum x1, waiting for transfers between devices, per_device(): relation_total = lax.psum(relation_term, ('left', 'right'))  232 us
    reduce_scatter x1, waiting for transfers between devices, per_device(): lax.psum_scatter(jnp.einsum('er,ed->rd', onehot, all_grads, preferred_ele...  175 us
    reduce_scatter x1, waiting for transfers between devices, per_device(): lax.psum_scatter(jnp.einsum('er,ed->rd', onehot, source_grad, preferred_e...  61.4 us
    all_gather x1, waiting for transfers between devices, per_device(): lax.all_gather(moved_table.astype(jnp.bfloat16), 'left', axis=0, tiled=True)  54 us
    all_to_all x1, waiting for transfers between devices, per_device(): lax.all_to_all(jnp.stack([left_table.astype(jnp.bfloat16)] * lax.axis_siz...  21.4 us
    gather x2, local copies, waits for them, and re-layouts, per_device(): negative_rows = jnp.take(right_part, negative, axis=0)  13.2 us
  transfers between devices with their start and end apart: 7, of which 6 were waited for; matrix products, arithmetic and copies ran while one was open for 4% of the time, Pallas kernels for 0%

profile of v1, /device:TPU:2, one launch (start us, length us, event | category | flops | bytes accessed | tf_op | source)
XLA Modules:
  0.0 633.5 jit_solution(17398613432050681578)
XLA Ops:
  7.3 5.4 collective-permute-done
  14.3 1.4 stack.2
  15.7 8.6 %all-to-all-start = ((bf16[16,128,400]{1,2,0:T(8,128)(2,1)}), bf16[16,128,400]{1,2,0:T(8,128)(2,1)}, u32[]{:S(2)}, u32[]{:S(2)}) async-start(bf16[16,128,400]{1,2,0:T(8,128)(2,1)} %stack.2), calls=%async_computation | async-start | bytes 3276800 | tf_op jit(solution)/shard_map/all_to_all | solution.py:62
  25.0 21.4 %all-to-all-done = bf16[16,128,400]{1,2,0:T(8,128)(2,1)} async-done(((bf16[16,128,400]{1,2,0:T(8,128)(2,1)}), bf16[16,128,400]{1,2,0:T(8,128)(2,1)}, u32[]{:S(2)}, u32[]{:S(2)}) %all-to-all-start) | async-done | bytes 1638432 | tf_op jit(solution)/shard_map/all_to_all | solution.py:62
  46.4 3.5 fusion.3
  50.0 1.5 fusion.36
  52.5 54.0 %all-gather.2.cloned.1.call-done = bf16[2048,400]{0,1:T(8,128)(2,1)} async-done(((bf16[128,400]{0,1:T(8,128)(2,1)}), bf16[2048,400]{0,1:T(8,128)(2,1)}) %all-gather.2.cloned.1.call-update) | async-done | bytes 1638416 | tf_op jit(solution)/shard_map/all_gather | solution.py:60
  106.5 2.8 copy.39
  109.3 9.2 %gather_fusion = bf16[2048,400]{1,0:T(8,128)(2,1)} fusion(bf16[2048,400]{1,0:T(8,128)(2,1)S(1)} %copy.39, s32[2048]{0:T(1024)S(1)} %bitcast_clamp_fusion), kind=kCustom, calls=%fused_computation | custom fusion | bytes 3284992 | tf_op jit(solution)/shard_map/jit(_take)/gather | solution.py:77
  118.4 4.1 copy.40
  122.5 2.2 multiply_reduce_fusion
  124.7 1.8 multiply_convert_fusion
  130.7 1.3 fusion.14
  132.2 3.9 fusion.2
  136.2 1.0 copy-done.12
  137.3 2.6 fusion.13
  140.0 7.8 %fusion = f32[2048,400]{0,1:T(8,128)} fusion(s32[3072]{0:T(1024)S(1)} %pad_add_fusion, bf16[2048,400]{0,1:T(8,128)(2,1)S(1)} %bitcast.45, bf16[1024,400]{0,1:T(8,128)(2,1)S(1)} %get-tuple-element.24), kind=kOutput, calls=%fused_computation.2 | convolution fusion | flops 5044371456 | bytes 5746688 | tf_op jit(solution)/shard_map/er,ed->rd/dot_general | solution.py:116
  148.5 232.4 %all-reduce.2.cloned.1.call-done = f32[256,400]{0,1:T(8,128)} async-done(((f32[256,400]{0,1:T(8,128)}), f32[256,400]{0,1:T(8,128)}) %all-reduce.2.cloned.1.call-update) | async-done | bytes 409616 | tf_op jit(solution)/shard_map/psum | solution.py:123
  380.9 1.1 multiply_reduce_fusion.1
  382.5 1.8 divide_subtract_fusion
  384.4 61.4 %reduce-scatter.3.cloned.1.call-done = f32[128,400]{0,1:T(8,128)} async-done(((f32[2048,400]{0,1:T(8,128)}), f32[128,400]{0,1:T(8,128)}) %reduce-scatter.3.cloned.1.call-update) | async-done | bytes 204816 | tf_op jit(solution)/shard_map/reduce_scatter | solution.py:106
  447.2 175.0 %reduce-scatter.5.cloned.1.call-done = f32[128,400]{0,1:T(8,128)} async-done(((f32[2048,400]{0,1:T(8,128)}), f32[128,400]{0,1:T(8,128)}) %reduce-scatter.5.cloned.1.call-update) | async-done | bytes 204816 | tf_op jit(solution)/shard_map/reduce_scatter | solution.py:115
  623.7 1.6 divide_subtract_fusion.1
  625.4 1.6 divide_subtract_fusion.2
  (73 shorter events, 12.1 us)
Async XLA Ops:
  7.2 99.3 %all-gather.2.cloned.1.call-start = ((), (), s32[]{:S(2)}) async-start(), calls=%async_computation.3 | async-start | bytes 1740800 | tf_op jit(solution)/shard_map/all_gather | solution.py:60
  7.2 5.5 collective-permute-start
  15.7 8.7 %copy-start.13 = (s32[1,1,2,1024]{3,2,1,0:T(2,128)S(1)}, s32[1,1,2,1024]{3,2,1,0:T(2,128)}, u32[]{:S(2)}) copy-start(s32[1,1,2,1024]{3,2,1,0:T(2,128)} %param.19) | copy-start | bytes 24580
  15.7 8.7 %copy-start.7 = (f32[256,400]{0,1:T(8,128)S(1)}, f32[256,400]{0,1:T(8,128)}, u32[]{:S(2)}) copy-start(f32[256,400]{0,1:T(8,128)} %param.14) | copy-start | bytes 1228804
  15.7 8.8 %copy-start.14 = (s32[1,1,1024]{2,1,0:T(1,128)S(1)}, s32[1,1,1024]{2,1,0:T(1,128)}, u32[]{:S(2)}) copy-start(s32[1,1,1024]{2,1,0:T(1,128)} %param.18) | copy-start | bytes 12292
  15.7 30.7 %all-to-all-start = ((bf16[16,128,400]{1,2,0:T(8,128)(2,1)}), bf16[16,128,400]{1,2,0:T(8,128)(2,1)}, u32[]{:S(2)}, u32[]{:S(2)}) async-start(bf16[16,128,400]{1,2,0:T(8,128)(2,1)} %stack.2), calls=%async_computation | async-start | bytes 3276800 | tf_op jit(solution)/shard_map/all_to_all | solution.py:62
  24.3 22.1 %copy-start.18 = (s32[1,1,1024]{2,1,0:T(1,128)S(1)}, s32[1,1,1024]{2,1,0:T(1,128)}, u32[]{:S(2)}) copy-start(s32[1,1,1024]{2,1,0:T(1,128)} %param.16) | copy-start | bytes 12292
  24.4 356.5 %all-reduce.2.cloned.1.call-start = ((), (), s32[]{:S(2)}) async-start(), calls=%async_computation.6 | async-start | bytes 819200 | tf_op jit(solution)/shard_map/psum | solution.py:123
  25.0 25.0 %copy-start = (f32[1024,400]{0,1:T(8,128)}, f32[1024,400]{0,1:T(8,128)S(1)}, u32[]{:S(2)}) copy-start(f32[1024,400]{0,1:T(8,128)S(1)} %fusion.15) | copy-start | bytes 4915204
  50.0 1.5 copy-start.2
  118.4 4.1 copy-start.4
  118.4 4.1 copy-start.5
  118.4 4.1 copy-start.15
  122.5 2.2 copy-start.6
  122.5 2.2 copy-start.11
  128.1 1.4 copy-start.1
  128.1 1.9 copy-start.3
  132.0 313.7 %reduce-scatter.3.cloned.1.call-start = ((), (), s32[]{:S(2)}) async-start(), calls=%async_computation.4 | async-start | bytes 3481600 | tf_op jit(solution)/shard_map/reduce_scatter | solution.py:106
  136.1 486.1 %reduce-scatter.5.cloned.1.call-start = ((), (), s32[]{:S(2)}) async-start(), calls=%async_computation.5 | async-start | bytes 3481600 | tf_op jit(solution)/shard_map/reduce_scatter | solution.py:115
  147.9 234.1 %copy-start.16 = (f32[256]{0:T(256)S(1)}, f32[256]{0:T(256)}, u32[]{:S(2)}) copy-start(f32[256]{0:T(256)} %param.15) | copy-start | bytes 3076
  147.9 234.7 %copy-start.8 = (f32[256,400]{0,1:T(8,128)S(1)}, f32[256,400]{0,1:T(8,128)}, u32[]{:S(2)}) copy-start(f32[256,400]{0,1:T(8,128)} %param.14) | copy-start | bytes 1228804
  148.5 298.2 %copy-start.17 = (f32[128]{0:T(128)S(1)}, f32[128]{0:T(128)}, u32[]{:S(2)}) copy-start(f32[128]{0:T(128)} %param.11) | copy-start | bytes 1540
  148.5 476.9 %copy-start.9 = (f32[128,400]{0,1:T(8,128)S(1)}, f32[128,400]{0,1:T(8,128)}, u32[]{:S(2)}) copy-start(f32[128,400]{0,1:T(8,128)} %param.10) | copy-start | bytes 614404
  148.5 474.7 %collective-permute-start.1 = (f32[128]{0:T(128)S(1)}, f32[128]{0:T(128)S(1)}, u32[]{:S(2)}, u32[]{:S(2)}) collective-permute-start(f32[128]{0:T(128)S(1)} %copy-done.19), channel_id=1, source_target_pairs={{0,1},{1,2},{2,3},{3,4},{4,5},{5,6},{6,7},{7,8},{8,9},{9,10},{10,1... | collective-permute-start | bytes 1544 | tf_op jit(solution)/shard_map/ppermute | solution.py:12
  (4 other events, 4.1 us)
Sparse Core Ops, SparseCore 0:
  13.5 92.9 all-gather.1
  132.1 248.7 all-reduce.1
  383.5 62.1 reduce-scatter.2
  449.5 172.6 reduce-scatter.4
